TPU v7x, 32 devices: a whole 2x2x4 slice. The times are simulated.
32 devices in a mesh: shard: 8 (over z, x), seq: 4 (over y, core).
Axes of the slice: x: 2, y: 2, z: 4, core: 2. Of those that a mesh axis runs over, the one named last changes fastest.
Arguments:
- tokens: bfloat16 [16, 2048, 768], P('shard', 'seq'), may hold values from -6 to 6
- cotangent: bfloat16 [16, 2048, 768], P('shard', 'seq'), may hold values from -6 to 6
- query_weight: bfloat16 [768, 768], P('shard'), may hold values from -0.21875 to 0.21875
- key_weight: bfloat16 [768, 768], P('shard'), may hold values from -0.21875 to 0.21875
- value_weight: bfloat16 [768, 768], P('shard'), may hold values from -0.21875 to 0.21875
- output_weight: bfloat16 [768, 768], P('shard'), may hold values from -0.875 to 0.875
- inner_weight: bfloat16 [768, 3072], P('shard'), may hold values from -0.21875 to 0.21875
- inner_bias: bfloat16 [3072], P('shard'), may hold values from -3 to 3
- outer_weight: bfloat16 [3072, 768], P('shard'), may hold values from -0.109375 to 0.109375
- first_gain: bfloat16 [768], P('shard'), may hold values from 0.25 to 1.75
- first_shift: bfloat16 [768], P('shard'), may hold values from -3 to 3
- second_gain: bfloat16 [768], P('shard'), may hold values from 0.25 to 1.75
- second_shift: bfloat16 [768], P('shard'), may hold values from -3 to 3
- doc_starts: int32 [16, 3], P('shard'), may hold values from 0 to 2047, as said below
- random_blocks: int32 [16, 32, 3], P('shard'), may hold values from 0 to 31
Outputs:
- layer_output: bfloat16 [16, 2048, 768], P('shard', 'seq')
- input_grad: bfloat16 [16, 2048, 768], P('shard', 'seq')
- query_grad: float32 [768, 768], P('shard')
- key_grad: float32 [768, 768], P('shard')
- value_grad: float32 [768, 768], P('shard')
- projection_grad: float32 [768, 768], P('shard')
- inner_grad: float32 [768, 3072], P('shard')
- inner_bias_grad: float32 [3072], P('shard')
- outer_grad: float32 [3072, 768], P('shard')
- first_gain_grad: float32 [768], P('shard')
- first_shift_grad: float32 [768], P('shard')
- second_gain_grad: float32 [768], P('shard')
- second_shift_grad: float32 [768], P('shard')
Inputs may be any that keep to these rules, and one draw needn't show every extreme that they name: `doc_starts`: each sequence has 3 distinct starts in increasing order, the first 0, all below 2048; the last start of the first sequence is 2047.
All inputs are finite; a program needn't handle non-finite values.
Results may differ from a plain program's by a relative error of at most 0.017.
Values may be sent and summed in bfloat16 or wider, within the bound.
No kernel may reach another device: no remote copies, remote signals or barrier semaphores. Data moves between devices by JAX's collectives and lax.ppermute only.
A program may use at most 320 MiB of HBM per device.

v0:
```python
import math
import jax
import jax.numpy as jnp
from jax import lax
from jax.sharding import PartitionSpec as P

H = 12
HD = 64
BLK = 64
EPS = 1e-06


def for_sending(array):

    def short(part):
        return part.astype(jnp.bfloat16) if part.dtype == jnp.float32 else part

    return jax.tree.map(short, array)


def layer_norm(values, gain, shift):
    centered = values - jnp.mean(values, axis=-1, keepdims=True)
    spread = jnp.mean(centered * centered, axis=-1, keepdims=True)
    return centered * lax.rsqrt(spread + EPS) * gain + shift


def activate(values):
    return jax.nn.gelu(values, approximate=True)


def block_mask(starts, chosen, seq_len, width):
    blocks = seq_len // width
    places = jnp.arange(seq_len, dtype=jnp.int32)
    segment = jnp.sum((starts[None, :] <= places[:, None]).astype(jnp.int32), axis=1)
    follow = jnp.concatenate([starts[1:], jnp.full((1,), seq_len, jnp.int32)])
    first_block = starts // width
    last_block = (follow - 1) // width
    numbers = jnp.arange(blocks, dtype=jnp.int32)
    special = jnp.any(first_block[None, :] == numbers[:, None], axis=1) | jnp.any(
        last_block[None, :] == numbers[:, None], axis=1
    )
    nearby = jnp.abs(numbers[:, None] - numbers[None, :]) <= 1
    picked = jnp.any(chosen[:, :, None] == numbers[None, None, :], axis=1)
    blocked = nearby | special[:, None] | special[None, :] | picked
    expanded = jnp.repeat(jnp.repeat(blocked, width, axis=0), width, axis=1)
    return expanded & (segment[:, None] == segment[None, :])


def body(
    tokens,
    cotangent,
    query_weight,
    key_weight,
    value_weight,
    output_weight,
    inner_weight,
    inner_bias,
    outer_weight,
    first_gain,
    first_shift,
    second_gain,
    second_shift,
    doc_starts,
    random_blocks,
):
    gathered = (
        lax.all_gather(query_weight, "shard", axis=0, tiled=True),
        lax.all_gather(key_weight, "shard", axis=0, tiled=True),
        lax.all_gather(value_weight, "shard", axis=0, tiled=True),
        lax.all_gather(output_weight, "shard", axis=0, tiled=True),
        lax.all_gather(inner_weight, "shard", axis=0, tiled=True),
        lax.all_gather(inner_bias, "shard", axis=0, tiled=True),
        lax.all_gather(outer_weight, "shard", axis=0, tiled=True),
        lax.all_gather(first_gain, "shard", axis=0, tiled=True),
        lax.all_gather(first_shift, "shard", axis=0, tiled=True),
        lax.all_gather(second_gain, "shard", axis=0, tiled=True),
        lax.all_gather(second_shift, "shard", axis=0, tiled=True),
    )
    (
        query_full,
        key_full,
        value_full,
        output_full,
        inner_full,
        bias_full,
        outer_full,
        gain_one,
        shift_one,
        gain_two,
        shift_two,
    ) = gathered
    width = query_full.shape[0]
    hidden = inner_full.shape[1]
    joined_weight = jnp.concatenate([query_full, key_full, value_full], axis=1)
    bias_float = bias_full.astype(jnp.float32)
    gain_one_f = gain_one.astype(jnp.float32)
    shift_one_f = shift_one.astype(jnp.float32)
    gain_two_f = gain_two.astype(jnp.float32)
    shift_two_f = shift_two.astype(jnp.float32)
    groups = lax.axis_size("seq")
    local_len = tokens.shape[1]
    seq_len = local_len * groups
    head_group = H // groups
    group_width = head_group * HD
    block_rows = min(512, seq_len)
    scale = 1.0 / math.sqrt(HD)

    def micro_step(totals, inputs):
        (
            acc_joined,
            acc_output,
            acc_inner,
            acc_bias,
            acc_outer,
            acc_gain_one,
            acc_shift_one,
            acc_gain_two,
            acc_shift_two,
        ) = totals
        row, grad_row, starts, chosen = inputs
        attend = block_mask(starts, chosen, seq_len, BLK)
        joined = jnp.dot(row, joined_weight, preferred_element_type=jnp.float32).astype(
            jnp.bfloat16
        )
        joined = joined.reshape(local_len, 3, groups, group_width)
        by_heads = lax.all_to_all(joined, "seq", split_axis=2, concat_axis=0, tiled=True).reshape(
            seq_len, 3, head_group, HD
        )
        queries = by_heads[:, 0]
        keys_all = by_heads[:, 1]
        values_all = by_heads[:, 2]

        def masked_scores(start):
            query_block = queries[start : start + block_rows]
            scores = (
                jnp.einsum(
                    "qhd,khd->hqk", query_block, keys_all, preferred_element_type=jnp.float32
                )
                * scale
            )
            return (
                query_block,
                jnp.where(attend[start : start + block_rows][None], scores, -1000000000.0),
            )

        contexts = []
        log_totals = []
        for start in range(0, seq_len, block_rows):
            query_block, scores = masked_scores(start)
            highest_score = jnp.max(scores, axis=-1, keepdims=True)
            expd = jnp.exp(scores - highest_score)
            denom = jnp.sum(expd, axis=-1, keepdims=True)
            probs = expd / denom
            log_totals.append(highest_score + jnp.log(denom))
            contexts.append(
                jnp.einsum(
                    "hqk,khd->qhd",
                    probs.astype(jnp.bfloat16),
                    values_all,
                    preferred_element_type=jnp.float32,
                ).astype(jnp.bfloat16)
            )
        context_heads = jnp.concatenate(contexts, axis=0).reshape(seq_len, 1, group_width)
        context = (
            lax.all_to_all(
                for_sending(context_heads), "seq", split_axis=0, concat_axis=1, tiled=True
            )
            .astype(context_heads.dtype)
            .reshape(local_len, width)
        )
        attended = jnp.dot(context, output_full, preferred_element_type=jnp.float32)
        res_one = row.astype(jnp.float32) + attended
        first = layer_norm(res_one, gain_one_f, shift_one_f)
        first_low = first.astype(jnp.bfloat16)
        inner = jnp.dot(first_low, inner_full, preferred_element_type=jnp.float32) + bias_float
        active = activate(inner).astype(jnp.bfloat16)
        outer = jnp.dot(active, outer_full, preferred_element_type=jnp.float32)
        res_two = first + outer
        result = layer_norm(res_two, gain_two_f, shift_two_f).astype(jnp.bfloat16)
        grad_float = grad_row.astype(jnp.float32)
        _, norm_two_back = jax.vjp(layer_norm, res_two, gain_two_f, shift_two_f)
        d_second, d_gain_two, d_shift_two = norm_two_back(grad_float)
        d_outer = d_second.astype(jnp.bfloat16)
        acc_outer = acc_outer + jnp.einsum(
            "ti,td->id", active, d_outer, preferred_element_type=jnp.float32
        )
        d_active = jnp.einsum("td,id->ti", d_outer, outer_full, preferred_element_type=jnp.float32)
        _, gelu_back = jax.vjp(activate, inner)
        d_inner = gelu_back(d_active)[0].astype(jnp.bfloat16)
        acc_bias = acc_bias + jnp.sum(d_inner.astype(jnp.float32), axis=0)
        acc_inner = acc_inner + jnp.einsum(
            "td,tf->df", first_low, d_inner, preferred_element_type=jnp.float32
        )
        d_first = d_second + jnp.einsum(
            "tf,df->td", d_inner, inner_full, preferred_element_type=jnp.float32
        )
        _, norm_one_back = jax.vjp(layer_norm, res_one, gain_one_f, shift_one_f)
        d_res, d_gain_one, d_shift_one = norm_one_back(d_first)
        d_attended = d_res.astype(jnp.bfloat16)
        acc_output = acc_output + jnp.einsum(
            "ti,td->id", context, d_attended, preferred_element_type=jnp.float32
        )
        d_context = jnp.einsum(
            "td,id->ti", d_attended, output_full, preferred_element_type=jnp.float32
        )
        d_context = d_context.astype(jnp.bfloat16).reshape(local_len, groups, group_width)
        d_heads = lax.all_to_all(d_context, "seq", split_axis=1, concat_axis=0, tiled=True).reshape(
            seq_len, head_group, HD
        )
        d_keys = jnp.zeros((seq_len, head_group, HD), jnp.float32)
        d_values = jnp.zeros((seq_len, head_group, HD), jnp.float32)
        d_query_blocks = []
        for index, start in enumerate(range(0, seq_len, block_rows)):
            query_block, scores = masked_scores(start)
            probs = jnp.exp(scores - log_totals[index])
            grad_block = d_heads[start : start + block_rows]
            d_probs = jnp.einsum(
                "qhd,khd->hqk", grad_block, values_all, preferred_element_type=jnp.float32
            )
            d_values = d_values + jnp.einsum(
                "hqk,qhd->khd",
                probs.astype(jnp.bfloat16),
                grad_block,
                preferred_element_type=jnp.float32,
            )
            centered = d_probs - jnp.sum(probs * d_probs, axis=-1, keepdims=True)
            d_scores = (probs * centered * scale).astype(jnp.bfloat16)
            d_query_blocks.append(
                jnp.einsum("hqk,khd->qhd", d_scores, keys_all, preferred_element_type=jnp.float32)
            )
            d_keys = d_keys + jnp.einsum(
                "hqk,qhd->khd", d_scores, query_block, preferred_element_type=jnp.float32
            )
        d_queries = jnp.concatenate(d_query_blocks, axis=0)
        d_joined = jnp.stack([d_queries, d_keys, d_values], axis=1).astype(jnp.bfloat16)
        d_joined = d_joined.reshape(seq_len, 3, 1, group_width)
        d_local = lax.all_to_all(d_joined, "seq", split_axis=0, concat_axis=2, tiled=True).reshape(
            local_len, 3 * width
        )
        acc_joined = acc_joined + jnp.einsum(
            "td,te->de", row, d_local, preferred_element_type=jnp.float32
        )
        d_input = d_res + jnp.einsum(
            "te,de->td", d_local, joined_weight, preferred_element_type=jnp.float32
        )
        updated = (
            acc_joined,
            acc_output,
            acc_inner,
            acc_bias,
            acc_outer,
            acc_gain_one + d_gain_one,
            acc_shift_one + d_shift_one,
            acc_gain_two + d_gain_two,
            acc_shift_two + d_shift_two,
        )
        return (updated, (result, d_input.astype(jnp.bfloat16)))

    starting = (
        jnp.zeros((width, 3 * width), jnp.float32),
        jnp.zeros((width, width), jnp.float32),
        jnp.zeros((width, hidden), jnp.float32),
        jnp.zeros((hidden,), jnp.float32),
        jnp.zeros((hidden, width), jnp.float32),
        jnp.zeros((width,), jnp.float32),
        jnp.zeros((width,), jnp.float32),
        jnp.zeros((width,), jnp.float32),
        jnp.zeros((width,), jnp.float32),
    )
    totals, (outputs, input_grads) = lax.scan(
        micro_step, starting, (tokens, cotangent, doc_starts, random_blocks)
    )
    (
        acc_joined,
        acc_output,
        acc_inner,
        acc_bias,
        acc_outer,
        acc_gain_one,
        acc_shift_one,
        acc_gain_two,
        acc_shift_two,
    ) = totals
    local_grads = (
        acc_joined[:, :width],
        acc_joined[:, width : 2 * width],
        acc_joined[:, 2 * width :],
        acc_output,
        acc_inner,
        acc_bias,
        acc_outer,
        acc_gain_one,
        acc_shift_one,
        acc_gain_two,
        acc_shift_two,
    )
    shares = (
        lax.psum_scatter(local_grads[0], "shard", scatter_dimension=0, tiled=True),
        lax.psum_scatter(local_grads[1], "shard", scatter_dimension=0, tiled=True),
        lax.psum_scatter(local_grads[2], "shard", scatter_dimension=0, tiled=True),
        lax.psum_scatter(local_grads[3], "shard", scatter_dimension=0, tiled=True),
        lax.psum_scatter(local_grads[4], "shard", scatter_dimension=0, tiled=True),
        lax.psum_scatter(local_grads[5], "shard", scatter_dimension=0, tiled=True),
        lax.psum_scatter(local_grads[6], "shard", scatter_dimension=0, tiled=True),
        lax.psum_scatter(local_grads[7], "shard", scatter_dimension=0, tiled=True),
        lax.psum_scatter(local_grads[8], "shard", scatter_dimension=0, tiled=True),
        lax.psum_scatter(local_grads[9], "shard", scatter_dimension=0, tiled=True),
        lax.psum_scatter(local_grads[10], "shard", scatter_dimension=0, tiled=True),
    )
    summed = (
        lax.psum(shares[0].astype(jnp.bfloat16), "seq").astype(jnp.float32),
        lax.psum(shares[1].astype(jnp.bfloat16), "seq").astype(jnp.float32),
        lax.psum(shares[2].astype(jnp.bfloat16), "seq").astype(jnp.float32),
        lax.psum(shares[3].astype(jnp.bfloat16), "seq").astype(jnp.float32),
        lax.psum(shares[4].astype(jnp.bfloat16), "seq").astype(jnp.float32),
        lax.psum(shares[5].astype(jnp.bfloat16), "seq").astype(jnp.float32),
        lax.psum(shares[6].astype(jnp.bfloat16), "seq").astype(jnp.float32),
        lax.psum(shares[7].astype(jnp.bfloat16), "seq").astype(jnp.float32),
        lax.psum(shares[8].astype(jnp.bfloat16), "seq").astype(jnp.float32),
        lax.psum(shares[9].astype(jnp.bfloat16), "seq").astype(jnp.float32),
        lax.psum(shares[10].astype(jnp.bfloat16), "seq").astype(jnp.float32),
    )
    return (
        outputs,
        input_grads,
        summed[0],
        summed[1],
        summed[2],
        summed[3],
        summed[4],
        summed[5],
        summed[6],
        summed[7],
        summed[8],
        summed[9],
        summed[10],
    )


def solution(mesh):
    placed = (
        P("shard", "seq", None),
        P("shard", "seq", None),
        P("shard", None),
        P("shard", None),
        P("shard", None),
        P("shard", None),
        P("shard", None),
        P("shard"),
        P("shard", None),
        P("shard"),
        P("shard"),
        P("shard"),
        P("shard"),
        P("shard", None),
        P("shard", None, None),
    )
    return jax.shard_map(
        body,
        mesh=mesh,
        in_specs=placed,
        out_specs=(
            P("shard", "seq", None),
            P("shard", "seq", None),
            P("shard", None),
            P("shard", None),
            P("shard", None),
            P("shard", None),
            P("shard", None),
            P("shard"),
            P("shard", None),
            P("shard"),
            P("shard"),
            P("shard"),
            P("shard"),
        ),
        check_vma=False,
    )
```

profile of v0, /device:TPU:0, one launch (start us, length us, event | category | flops | bytes accessed | tf_op | source)
XLA Modules:
  0.0 2124.0 jit_solution(12101311446130389150)
XLA Ops:
  17.3 23.5 %all-reduce.10 = (bf16[768]{0:T(1024)(128)(2,1)S(1)}, bf16[768]{0:T(1024)(128)(2,1)S(1)}, bf16[768]{0:T(1024)(128)(2,1)S(1)}, bf16[768]{0:T(1024)(128)(2,1)S(1)}) all-reduce(bf16[768]{0:T(1024)(128)(2,1)S(1)} %dynamic-update-slice, bf16[768]{0:T(1024)(128)(2,1)S(1)} %dynamic-update-slice.1, ...), channel_id=1, replica_groups=mesh['shard'=8,'seq'=4] {'shard'}, use_global_device_ids=true, to_apply=%add | all-reduce | flops 3072 | bytes 12288
  41.4 26.0 %all-gather = bf16[8,1,384]{2,1,0:T(2,128)(2,1)S(1)} all-gather(bf16[1,1,384]{2,1,0:T(2,128)(2,1)S(1)} %reshape.380), channel_id=1, replica_groups=mesh['shard'=8,'seq'=4] {'shard'}, dimensions={0}, use_global_device_ids=true | all-gather | bytes 6912 | tf_op jit(solution)/shard_map/all_gather | solution.py:72
  67.5 28.6 %all-gather.10.cloned.1.call-done = bf16[768,768]{1,0:T(8,128)(2,1)} async-done(((bf16[96,768]{1,0:T(8,128)(2,1)}), bf16[768,768]{1,0:T(8,128)(2,1)}) %all-gather.10.cloned.1.call-update) | async-done | bytes 1179664 | tf_op jit(solution)/shard_map/all_gather | solution.py:68
  96.1 42.0 %all-gather.12.cloned.1.call-done = bf16[768,768]{1,0:T(8,128)(2,1)} async-done(((bf16[96,768]{1,0:T(8,128)(2,1)}), bf16[768,768]{1,0:T(8,128)(2,1)}) %all-gather.12.cloned.1.call-update) | async-done | bytes 1179664 | tf_op jit(solution)/shard_map/all_gather | solution.py:69
  141.4 38.6 %all-gather.14.cloned.1.call-done = bf16[768,768]{1,0:T(8,128)(2,1)} async-done(((bf16[96,768]{1,0:T(8,128)(2,1)}), bf16[768,768]{1,0:T(8,128)(2,1)}) %all-gather.14.cloned.1.call-update) | async-done | bytes 1179664 | tf_op jit(solution)/shard_map/all_gather | solution.py:70
  180.0 80.1 %all-gather.16.cloned.1.call-done = bf16[768,3072]{1,0:T(8,128)(2,1)} async-done(((bf16[96,3072]{1,0:T(8,128)(2,1)}), bf16[768,3072]{1,0:T(8,128)(2,1)}) %all-gather.16.cloned.1.call-update) | async-done | bytes 4718608 | tf_op jit(solution)/shard_map/all_gather | solution.py:71
  260.1 79.8 %all-gather.18.cloned.1.call-done = bf16[3072,768]{1,0:T(8,128)(2,1)} async-done(((bf16[384,768]{1,0:T(8,128)(2,1)}), bf16[3072,768]{1,0:T(8,128)(2,1)}) %all-gather.18.cloned.1.call-update) | async-done | bytes 4718608 | tf_op jit(solution)/shard_map/all_gather | solution.py:73
  339.8 1103.4 %while.34 = (s32[]{:T(128)}, f32[768,2304]{1,0:T(8,128)}, f32[768,768]{1,0:T(8,128)}, f32[768,3072]{1,0:T(8,128)}, f32[3072]{0:T(1024)}, /*index=5*/f32[3072,768...) while((s32[]{:T(128)}, f32[768,2304]{1,0:T(8,128)}, ...), condition=%wide.region_30.31_spmd.clone, body=%wide.region_0.30_spmd.clone.sunk | while | flops 32024104960 | bytes 1287496960 | solution.py:270
  550.3 23.6 %fusion.482 = bf16[512,3,64]{0,2,1:T(8,128)(2,1)} fusion(f32[3,512,2048]{2,1,0:T(8,128)} %fusion.471, f32[3,512,2048]{2,1,0:T(8,128)} %get-tuple-element.919, f32[3,512]{1,0:T(4,128)S(1)} %log_add_fusion.10, pred[512,2048]{1,0:T(8,128)(4,1)} %copy.126, bf16[2048,3,3,64]{0,3,2,1:T(8,128)(2,1)S(1)} %copy-done.2), kind=kOutput, calls=%fused_computation.156.clone.1 | convolution fusion | flops 437358080 | bytes 53428224 | tf_op jit(solution)/shard_map/while/body/eval_jaxpr/hqk,khd->qhd/dot_general | solution.py:229
  573.9 27.8 %fusion.472 = f32[3,64,2048]{2,1,0:T(8,128)} fusion(f32[3,512,2048]{2,1,0:T(8,128)} %fusion.471, f32[3,512,2048]{2,1,0:T(8,128)} %get-tuple-element.919, f32[3,512]{1,0:T(4,128)S(1)} %log_add_fusion.10, pred[512,2048]{1,0:T(8,128)(4,1)} %copy.126, bf16[2048,3,3,64]{0,3,2,1:T(8,128)(2,1)S(1)} %copy-done.2), kind=kOutput, calls=%fused_computation.47.clone.1 | convolution fusion | flops 437259776 | bytes 54214656 | tf_op jit(solution)/shard_map/while/body/eval_jaxpr/hqk,qhd->khd/dot_general | solution.py:231
  649.1 20.8 fusion.479
  669.8 23.9 %fusion.480 = bf16[512,3,64]{0,2,1:T(8,128)(2,1)} fusion(f32[3,512,2048]{2,1,0:T(8,128)} %fusion.475, f32[3,512,2048]{2,1,0:T(8,128)} %get-tuple-element.913, f32[3,512]{1,0:T(4,128)S(1)} %log_add_fusion.8, pred[512,2048]{1,0:T(8,128)(4,1)} %copy.124, bf16[2048,3,3,64]{0,3,2,1:T(8,128)(2,1)S(1)} %copy-done.2), kind=kOutput, calls=%fused_computation.158.clone.1 | convolution fusion | flops 437358080 | bytes 53428224 | tf_op jit(solution)/shard_map/while/body/eval_jaxpr/hqk,khd->qhd/dot_general | solution.py:229
  693.7 24.0 %fusion.481 = bf16[512,3,64]{0,2,1:T(8,128)(2,1)} fusion(f32[3,512,2048]{2,1,0:T(8,128)} %fusion.473, f32[3,512,2048]{2,1,0:T(8,128)} %get-tuple-element.916, f32[3,512]{1,0:T(4,128)S(1)} %log_add_fusion.9, pred[512,2048]{1,0:T(8,128)(4,1)} %copy.125, bf16[2048,3,3,64]{0,3,2,1:T(8,128)(2,1)S(1)} %copy-done.2), kind=kOutput, calls=%fused_computation.157.clone.1 | convolution fusion | flops 437358080 | bytes 53428224 | tf_op jit(solution)/shard_map/while/body/eval_jaxpr/hqk,khd->qhd/dot_general | solution.py:229
  717.7 25.7 %fusion.474 = f32[3,64,2048]{2,1,0:T(8,128)} fusion(f32[3,64,2048]{2,1,0:T(8,128)} %fusion.472, f32[3,512,2048]{2,1,0:T(8,128)} %fusion.473, f32[3,512,2048]{2,1,0:T(8,128)} %get-tuple-element.916, f32[3,512]{1,0:T(4,128)S(1)} %log_add_fusion.9, pred[512,2048]{1,0:T(8,128)(4,1)} %copy.125, bf16[2048,3,3,64]{0,3,2,1:T(8,128)(2,1)S(1)} %copy-done.2), kind=kOutput, calls=%fused_computation.118.clone.1 | convolution fusion | flops 437652992 | bytes 55787520 | tf_op jit(solution)/shard_map/while/body/eval_jaxpr/hqk,qhd->khd/dot_general | solution.py:231
  743.4 26.0 %fusion.476 = f32[3,64,2048]{2,1,0:T(8,128)} fusion(f32[3,64,2048]{2,1,0:T(8,128)} %fusion.474, f32[3,512,2048]{2,1,0:T(8,128)} %fusion.475, f32[3,512,2048]{2,1,0:T(8,128)} %get-tuple-element.913, f32[3,512]{1,0:T(4,128)S(1)} %log_add_fusion.8, pred[512,2048]{1,0:T(8,128)(4,1)} %copy.124, bf16[2048,3,3,64]{0,3,2,1:T(8,128)(2,1)S(1)} %copy-done.2), kind=kOutput, calls=%fused_computation.117.clone.1 | convolution fusion | flops 437652992 | bytes 55787520 | tf_op jit(solution)/shard_map/while/body/eval_jaxpr/hqk,qhd->khd/dot_general | solution.py:231
  769.4 22.3 %fusion.478 = bf16[3,64,2048]{2,1,0:T(8,128)(2,1)} fusion(f32[3,64,2048]{2,1,0:T(8,128)} %fusion.476, f32[3,512,2048]{2,1,0:T(8,128)} %fusion.477, f32[3,512,2048]{2,1,0:T(8,128)} %get-tuple-element.910, f32[3,512]{1,0:T(4,128)S(1)} %log_add_fusion.11, pred[512,2048]{1,0:T(8,128)(4,1)S(1)} %copy-done.7, bf16[2048,3,3,64]{0,3,2,1:T(8,128)(2,1)S(1)} %copy-done.2), kind=kOutput, calls=%fused_computation.119.clone.1 | convolution fusion | flops 438046208 | bytes 55001088 | tf_op jit(solution)/shard_map/while/body/eval_jaxpr/hqk,qhd->khd/dot_general | solution.py:231
  830.7 35.7 %all-to-all-done.3 = bf16[2048,3,1,192]{3,1,2,0:T(4,128)(2,1)} async-done(((bf16[2048,3,1,192]{3,1,2,0:T(4,128)(2,1)}), bf16[2048,3,1,192]{3,1,2,0:T(4,128)(2,1)}, u32[]{:S(2)}, u32[]{:S(2)}) %all-to-all-start.3) | async-done | bytes 2359328 | tf_op jit(solution)/shard_map/while/body/eval_jaxpr/all_to_all | solution.py:237
  1100.7 23.6 %fusion.482 = bf16[512,3,64]{0,2,1:T(8,128)(2,1)} fusion(f32[3,512,2048]{2,1,0:T(8,128)} %fusion.471, f32[3,512,2048]{2,1,0:T(8,128)} %get-tuple-element.919, f32[3,512]{1,0:T(4,128)S(1)} %log_add_fusion.10, pred[512,2048]{1,0:T(8,128)(4,1)} %copy.126, bf16[2048,3,3,64]{0,3,2,1:T(8,128)(2,1)S(1)} %copy-done.2), kind=kOutput, calls=%fused_computation.156.clone.1 | convolution fusion | flops 437358080 | bytes 53428224 | tf_op jit(solution)/shard_map/while/body/eval_jaxpr/hqk,khd->qhd/dot_general | solution.py:229
  1124.3 28.0 %fusion.472 = f32[3,64,2048]{2,1,0:T(8,128)} fusion(f32[3,512,2048]{2,1,0:T(8,128)} %fusion.471, f32[3,512,2048]{2,1,0:T(8,128)} %get-tuple-element.919, f32[3,512]{1,0:T(4,128)S(1)} %log_add_fusion.10, pred[512,2048]{1,0:T(8,128)(4,1)} %copy.126, bf16[2048,3,3,64]{0,3,2,1:T(8,128)(2,1)S(1)} %copy-done.2), kind=kOutput, calls=%fused_computation.47.clone.1 | convolution fusion | flops 437259776 | bytes 54214656 | tf_op jit(solution)/shard_map/while/body/eval_jaxpr/hqk,qhd->khd/dot_general | solution.py:231
  1220.5 23.9 %fusion.480 = bf16[512,3,64]{0,2,1:T(8,128)(2,1)} fusion(f32[3,512,2048]{2,1,0:T(8,128)} %fusion.475, f32[3,512,2048]{2,1,0:T(8,128)} %get-tuple-element.913, f32[3,512]{1,0:T(4,128)S(1)} %log_add_fusion.8, pred[512,2048]{1,0:T(8,128)(4,1)} %copy.124, bf16[2048,3,3,64]{0,3,2,1:T(8,128)(2,1)S(1)} %copy-done.2), kind=kOutput, calls=%fused_computation.158.clone.1 | convolution fusion | flops 437358080 | bytes 53428224 | tf_op jit(solution)/shard_map/while/body/eval_jaxpr/hqk,khd->qhd/dot_general | solution.py:229
  1244.3 23.8 %fusion.481 = bf16[512,3,64]{0,2,1:T(8,128)(2,1)} fusion(f32[3,512,2048]{2,1,0:T(8,128)} %fusion.473, f32[3,512,2048]{2,1,0:T(8,128)} %get-tuple-element.916, f32[3,512]{1,0:T(4,128)S(1)} %log_add_fusion.9, pred[512,2048]{1,0:T(8,128)(4,1)} %copy.125, bf16[2048,3,3,64]{0,3,2,1:T(8,128)(2,1)S(1)} %copy-done.2), kind=kOutput, calls=%fused_computation.157.clone.1 | convolution fusion | flops 437358080 | bytes 53428224 | tf_op jit(solution)/shard_map/while/body/eval_jaxpr/hqk,khd->qhd/dot_general | solution.py:229
  1268.2 25.7 %fusion.474 = f32[3,64,2048]{2,1,0:T(8,128)} fusion(f32[3,64,2048]{2,1,0:T(8,128)} %fusion.472, f32[3,512,2048]{2,1,0:T(8,128)} %fusion.473, f32[3,512,2048]{2,1,0:T(8,128)} %get-tuple-element.916, f32[3,512]{1,0:T(4,128)S(1)} %log_add_fusion.9, pred[512,2048]{1,0:T(8,128)(4,1)} %copy.125, bf16[2048,3,3,64]{0,3,2,1:T(8,128)(2,1)S(1)} %copy-done.2), kind=kOutput, calls=%fused_computation.118.clone.1 | convolution fusion | flops 437652992 | bytes 55787520 | tf_op jit(solution)/shard_map/while/body/eval_jaxpr/hqk,qhd->khd/dot_general | solution.py:231
  1293.9 26.0 %fusion.476 = f32[3,64,2048]{2,1,0:T(8,128)} fusion(f32[3,64,2048]{2,1,0:T(8,128)} %fusion.474, f32[3,512,2048]{2,1,0:T(8,128)} %fusion.475, f32[3,512,2048]{2,1,0:T(8,128)} %get-tuple-element.913, f32[3,512]{1,0:T(4,128)S(1)} %log_add_fusion.8, pred[512,2048]{1,0:T(8,128)(4,1)} %copy.124, bf16[2048,3,3,64]{0,3,2,1:T(8,128)(2,1)S(1)} %copy-done.2), kind=kOutput, calls=%fused_computation.117.clone.1 | convolution fusion | flops 437652992 | bytes 55787520 | tf_op jit(solution)/shard_map/while/body/eval_jaxpr/hqk,qhd->khd/dot_general | solution.py:231
  1319.9 22.5 %fusion.478 = bf16[3,64,2048]{2,1,0:T(8,128)(2,1)} fusion(f32[3,64,2048]{2,1,0:T(8,128)} %fusion.476, f32[3,512,2048]{2,1,0:T(8,128)} %fusion.477, f32[3,512,2048]{2,1,0:T(8,128)} %get-tuple-element.910, f32[3,512]{1,0:T(4,128)S(1)} %log_add_fusion.11, pred[512,2048]{1,0:T(8,128)(4,1)S(1)} %copy-done.7, bf16[2048,3,3,64]{0,3,2,1:T(8,128)(2,1)S(1)} %copy-done.2), kind=kOutput, calls=%fused_computation.119.clone.1 | convolution fusion | flops 438046208 | bytes 55001088 | tf_op jit(solution)/shard_map/while/body/eval_jaxpr/hqk,qhd->khd/dot_general | solution.py:231
  1385.8 31.3 %all-to-all-done.3 = bf16[2048,3,1,192]{3,1,2,0:T(4,128)(2,1)} async-done(((bf16[2048,3,1,192]{3,1,2,0:T(4,128)(2,1)}), bf16[2048,3,1,192]{3,1,2,0:T(4,128)(2,1)}, u32[]{:S(2)}, u32[]{:S(2)}) %all-to-all-start.3) | async-done | bytes 2359328 | tf_op jit(solution)/shard_map/while/body/eval_jaxpr/all_to_all | solution.py:237
  1452.2 58.3 %reduce-scatter.13.cloned.1.call-done = f32[96,768]{1,0:T(8,128)} async-done(((f32[768,768]{1,0:T(8,128)}), f32[96,768]{1,0:T(8,128)}) %reduce-scatter.13.cloned.1.call-update) | async-done | bytes 294928 | tf_op jit(solution)/shard_map/reduce_scatter | solution.py:301
  1512.1 70.6 %reduce-scatter.11.cloned.1.call-done = f32[96,768]{1,0:T(8,128)} async-done(((f32[768,768]{1,0:T(8,128)}), f32[96,768]{1,0:T(8,128)}) %reduce-scatter.11.cloned.1.call-update) | async-done | bytes 294928 | tf_op jit(solution)/shard_map/reduce_scatter | solution.py:300
  1584.4 70.7 %reduce-scatter.7.cloned.1.call-done = f32[96,768]{1,0:T(8,128)} async-done(((f32[768,768]{1,0:T(8,128)}), f32[96,768]{1,0:T(8,128)}) %reduce-scatter.7.cloned.1.call-update) | async-done | bytes 294928 | tf_op jit(solution)/shard_map/reduce_scatter | solution.py:298
  1656.7 70.5 %reduce-scatter.9.cloned.1.call-done = f32[96,768]{1,0:T(8,128)} async-done(((f32[768,768]{1,0:T(8,128)}), f32[96,768]{1,0:T(8,128)}) %reduce-scatter.9.cloned.1.call-update) | async-done | bytes 294928 | tf_op jit(solution)/shard_map/reduce_scatter | solution.py:299
  1728.9 163.3 %reduce-scatter.15.cloned.1.call-done = f32[96,3072]{1,0:T(8,128)} async-done(((f32[768,3072]{1,0:T(8,128)}), f32[96,3072]{1,0:T(8,128)}) %reduce-scatter.15.cloned.1.call-update) | async-done | bytes 1179664 | tf_op jit(solution)/shard_map/reduce_scatter | solution.py:302
  1894.3 162.5 %reduce-scatter.17.cloned.1.call-done = f32[384,768]{1,0:T(8,128)} async-done(((f32[3072,768]{1,0:T(8,128)}), f32[384,768]{1,0:T(8,128)}) %reduce-scatter.17.cloned.1.call-update) | async-done | bytes 1179664 | tf_op jit(solution)/shard_map/reduce_scatter | solution.py:304
  2060.4 35.2 %all-reduce.9 = (bf16[3072]{0:T(1024)(128)(2,1)S(1)}, bf16[768]{0:T(1024)(128)(2,1)S(1)}, bf16[768]{0:T(1024)(128)(2,1)S(1)}, bf16[768]{0:T(1024)(128)(2,1)S(1)}, bf16[768]{0:T(1024)(128)(2,1)S(1)}) all-reduce(f32[3072]{0:T(1024)S(1)} %copy-done.26, f32[768]{0:T(1024)S(1)} %copy-done.40, ...), channel_id=7, replica_groups=mesh['shard'=8,'seq'=4] {'shard'}, use_global_device_ids=true, to_apply=%region_41.42.clone | all-reduce | flops 6144 | bytes 36864
  (506 shorter events, 718.6 us)
Async XLA Ops:
  7.2 60.3 %all-gather.8.cloned.1.call-start = ((), (), s32[]{:S(2)}) async-start(), calls=%async_computation.10 | async-start | bytes 1327104 | tf_op jit(solution)/shard_map/all_gather | solution.py:67
  7.9 88.2 %all-gather.10.cloned.1.call-start = ((), (), s32[]{:S(2)}) async-start(), calls=%async_computation.11 | async-start | bytes 1327104 | tf_op jit(solution)/shard_map/all_gather | solution.py:68
  8.7 129.4 %all-gather.12.cloned.1.call-start = ((), (), s32[]{:S(2)}) async-start(), calls=%async_computation.12 | async-start | bytes 1327104 | tf_op jit(solution)/shard_map/all_gather | solution.py:69
  9.4 170.6 %all-gather.14.cloned.1.call-start = ((), (), s32[]{:S(2)}) async-start(), calls=%async_computation.13 | async-start | bytes 1327104 | tf_op jit(solution)/shard_map/all_gather | solution.py:70
  10.0 250.1 %all-gather.16.cloned.1.call-start = ((), (), s32[]{:S(2)}) async-start(), calls=%async_computation.14 | async-start | bytes 5308416 | tf_op jit(solution)/shard_map/all_gather | solution.py:71
  10.6 329.3 %all-gather.18.cloned.1.call-start = ((), (), s32[]{:S(2)}) async-start(), calls=%async_computation.15 | async-start | bytes 5308416 | tf_op jit(solution)/shard_map/all_gather | solution.py:73
  11.1 1499.4 %reduce-scatter.13.cloned.1.call-start = ((), (), s32[]{:S(2)}) async-start(), calls=%async_computation.19 | async-start | bytes 2654208 | tf_op jit(solution)/shard_map/reduce_scatter | solution.py:301
  350.1 32.1 %all-to-all-start = ((bf16[512,3,4,192]{0,3,1,2:T(8,128)(2,1)}), bf16[512,3,4,192]{0,3,1,2:T(8,128)(2,1)S(1)}, u32[]{:S(2)}, u32[]{:S(2)}) async-start(bf16[512,3,4,192]{0,3,1,2:T(8,128)(2,1)} %copy.122), calls=%async_computation | async-start | bytes 4718592 | tf_op jit(solution)/shard_map/while/body/eval_jaxpr/all_to_all | solution.py:126
  365.7 97.7 %copy-start.6 = (pred[512,2048]{1,0:T(8,128)(4,1)}, pred[512,2048]{1,0:T(8,128)(4,1)S(1)}, u32[]{:S(2)}) copy-start(pred[512,2048]{1,0:T(8,128)(4,1)S(1)} %copy.120) | copy-start | bytes 3145732 | tf_op jit(solution)/shard_map/while
  390.2 73.2 %copy-start.1 = (bf16[2048,3,3,64]{0,3,2,1:T(8,128)(2,1)}, bf16[2048,3,3,64]{0,3,2,1:T(8,128)(2,1)S(1)}, u32[]{:S(2)}) copy-start(bf16[2048,3,3,64]{0,3,2,1:T(8,128)(2,1)S(1)} %reshape.411) | copy-start | bytes 7077892 | tf_op jit(solution)/shard_map/while
  474.8 15.1 all-to-all-start.1
  524.8 15.9 all-to-all-start.2
  542.0 82.7 %copy-start.20 = (bf16[1,512,1,192]{1,3,0,2:T(8,128)(2,1)}, bf16[1,512,1,192]{1,3,0,2:T(8,128)(2,1)S(1)}, u32[]{:S(2)}) copy-start(bf16[1,512,1,192]{1,3,0,2:T(8,128)(2,1)S(1)} %get-tuple-element.936) | copy-start | bytes 589828 | tf_op jit(solution)/shard_map/while
  813.0 53.4 %all-to-all-start.3 = ((bf16[2048,3,1,192]{3,1,2,0:T(4,128)(2,1)}), bf16[2048,3,1,192]{3,1,2,0:T(4,128)(2,1)}, u32[]{:S(2)}, u32[]{:S(2)}) async-start(bf16[2048,3,1,192]{3,1,2,0:T(4,128)(2,1)} %pad_maximum_fusion.9), calls=%async_computation.3 | async-start | bytes 8388608 | tf_op jit(solution)/shard_map/while/body/eval_jaxpr/all_to_all | solution.py:237
  900.7 32.1 %all-to-all-start = ((bf16[512,3,4,192]{0,3,1,2:T(8,128)(2,1)}), bf16[512,3,4,192]{0,3,1,2:T(8,128)(2,1)S(1)}, u32[]{:S(2)}, u32[]{:S(2)}) async-start(bf16[512,3,4,192]{0,3,1,2:T(8,128)(2,1)} %copy.122), calls=%async_computation | async-start | bytes 4718592 | tf_op jit(solution)/shard_map/while/body/eval_jaxpr/all_to_all | solution.py:126
  916.3 97.7 %copy-start.6 = (pred[512,2048]{1,0:T(8,128)(4,1)}, pred[512,2048]{1,0:T(8,128)(4,1)S(1)}, u32[]{:S(2)}) copy-start(pred[512,2048]{1,0:T(8,128)(4,1)S(1)} %copy.120) | copy-start | bytes 3145732 | tf_op jit(solution)/shard_map/while
  940.8 73.3 %copy-start.1 = (bf16[2048,3,3,64]{0,3,2,1:T(8,128)(2,1)}, bf16[2048,3,3,64]{0,3,2,1:T(8,128)(2,1)S(1)}, u32[]{:S(2)}) copy-start(bf16[2048,3,3,64]{0,3,2,1:T(8,128)(2,1)S(1)} %reshape.411) | copy-start | bytes 7077892 | tf_op jit(solution)/shard_map/while
  1025.4 15.1 all-to-all-start.1
  1075.3 15.9 all-to-all-start.2
  1092.5 82.9 %copy-start.20 = (bf16[1,512,1,192]{1,3,0,2:T(8,128)(2,1)}, bf16[1,512,1,192]{1,3,0,2:T(8,128)(2,1)S(1)}, u32[]{:S(2)}) copy-start(bf16[1,512,1,192]{1,3,0,2:T(8,128)(2,1)S(1)} %get-tuple-element.936) | copy-start | bytes 589828 | tf_op jit(solution)/shard_map/while
  1363.7 53.3 %all-to-all-start.3 = ((bf16[2048,3,1,192]{3,1,2,0:T(4,128)(2,1)}), bf16[2048,3,1,192]{3,1,2,0:T(4,128)(2,1)}, u32[]{:S(2)}, u32[]{:S(2)}) async-start(bf16[2048,3,1,192]{3,1,2,0:T(4,128)(2,1)} %pad_maximum_fusion.9), calls=%async_computation.3 | async-start | bytes 8388608 | tf_op jit(solution)/shard_map/while/body/eval_jaxpr/all_to_all | solution.py:237
  1443.2 139.6 %reduce-scatter.11.cloned.1.call-start = ((), (), s32[]{:S(2)}) async-start(), calls=%async_computation.18 | async-start | bytes 2654208 | tf_op jit(solution)/shard_map/reduce_scatter | solution.py:300
  1449.5 205.6 %reduce-scatter.7.cloned.1.call-start = ((), (), s32[]{:S(2)}) async-start(), calls=%async_computation.16 | async-start | bytes 2654208 | tf_op jit(solution)/shard_map/reduce_scatter | solution.py:298
  1450.3 277.0 %reduce-scatter.9.cloned.1.call-start = ((), (), s32[]{:S(2)}) async-start(), calls=%async_computation.17 | async-start | bytes 2654208 | tf_op jit(solution)/shard_map/reduce_scatter | solution.py:299
  1450.8 441.3 %reduce-scatter.15.cloned.1.call-start = ((), (), s32[]{:S(2)}) async-start(), calls=%async_computation.20 | async-start | bytes 10616832 | tf_op jit(solution)/shard_map/reduce_scatter | solution.py:302
  1451.6 605.3 %reduce-scatter.17.cloned.1.call-start = ((), (), s32[]{:S(2)}) async-start(), calls=%async_computation.21 | async-start | bytes 10616832 | tf_op jit(solution)/shard_map/reduce_scatter | solution.py:304
  1451.6 608.7 %copy-start.26 = (f32[3072]{0:T(1024)S(1)}, f32[3072]{0:T(1024)}, u32[]{:S(2)}) copy-start(f32[3072]{0:T(1024)} %get-tuple-element.396) | copy-start | bytes 36868
  1451.6 608.7 %copy-start.31 = (f32[768]{0:T(1024)S(1)}, f32[768]{0:T(1024)}, u32[]{:S(2)}) copy-start(f32[768]{0:T(1024)} %get-tuple-element.401) | copy-start | bytes 9220
  1451.6 608.7 %copy-start.34 = (f32[768]{0:T(1024)S(1)}, f32[768]{0:T(1024)}, u32[]{:S(2)}) copy-start(f32[768]{0:T(1024)} %get-tuple-element.400) | copy-start | bytes 9220
  1451.7 608.7 %copy-start.37 = (f32[768]{0:T(1024)S(1)}, f32[768]{0:T(1024)}, u32[]{:S(2)}) copy-start(f32[768]{0:T(1024)} %get-tuple-element.399) | copy-start | bytes 9220
  1451.7 608.7 %copy-start.40 = (f32[768]{0:T(1024)S(1)}, f32[768]{0:T(1024)}, u32[]{:S(2)}) copy-start(f32[768]{0:T(1024)} %get-tuple-element.398) | copy-start | bytes 9220
  1452.2 654.1 %all-reduce.15.cloned.1.call-start = ((), (), s32[]{:S(2)}) async-start(), calls=%async_computation.22 | async-start | bytes 3538944 | tf_op jit(solution)/shard_map/psum | solution.py:311
  (94 other events, 747.1 us)
Sparse Core Ops, SparseCore 0:
  10.2 43.8 all-gather.7
  56.2 39.8 all-gather.9
  98.3 39.8 all-gather.11
  140.1 39.8 all-gather.13
  182.0 78.0 all-gather.15
  262.1 77.6 all-gather.17
  1443.3 67.1 reduce-scatter.12
  1514.0 68.7 reduce-scatter.10
  1586.3 68.7 reduce-scatter.6
  1658.4 68.7 reduce-scatter.8
  1730.8 161.3 reduce-scatter.14
  1895.6 161.1 reduce-scatter.16
  2060.8 45.3 all-reduce.14
where the time goes:
time: 2130 us; the launch traced here: 2120 us
  waiting for transfers between devices  973 us (46%)
  matrix products  720 us (34%)
  local copies, waits for them, and re-layouts  156 us (7%)
  other arithmetic  130 us (6%)
  blocking collectives  91.2 us (4%)
  starting transfers between devices  33.5 us (2%)
    dot_general x8, matrix products, micro_step(): jnp.einsum('hqk,qhd->khd', d_scores, query_block, preferred_element_type=...  204 us
    dot_general x8, matrix products, micro_step(): jnp.einsum('hqk,khd->qhd', d_scores, keys_all, preferred_element_type=jnp...  184 us
    reduce_scatter x1, waiting for transfers between devices, body(): lax.psum_scatter(local_grads[4], 'shard', scatter_dimension=0, tiled=True)  163 us
    reduce_scatter x1, waiting for transfers between devices, body(): lax.psum_scatter(local_grads[6], 'shard', scatter_dimension=0, tiled=True)  163 us
    all_gather x1, waiting for transfers between devices, body(): lax.all_gather(inner_weight, 'shard', axis=0, tiled=True)  80.1 us
    all_gather x1, waiting for transfers between devices, body(): lax.all_gather(outer_weight, 'shard', axis=0, tiled=True)  79.8 us
    reduce_scatter x1, waiting for transfers between devices, body(): lax.psum_scatter(local_grads[0], 'shard', scatter_dimension=0, tiled=True)  70.7 us
    reduce_scatter x1, waiting for transfers between devices, body(): lax.psum_scatter(local_grads[2], 'shard', scatter_dimension=0, tiled=True)  70.6 us
  transfers between devices with their start and end apart: 21, of which 20 were waited for; matrix products, arithmetic and copies ran while one was open for 6% of the time, Pallas kernels for 0%

commit v1 on v0

--- a/solution.py
+++ b/solution.py
@@ -234,9 +234,12 @@
         d_queries = jnp.concatenate(d_query_blocks, axis=0)
         d_joined = jnp.stack([d_queries, d_keys, d_values], axis=1).astype(jnp.bfloat16)
         d_joined = d_joined.reshape(seq_len, 3, 1, group_width)
-        d_local = lax.all_to_all(d_joined, "seq", split_axis=0, concat_axis=2, tiled=True).reshape(
-            local_len, 3 * width
-        )
+        d_local = jnp.concatenate(
+            lax.all_to_all(
+                jnp.stack(jnp.split(d_joined, lax.axis_size("seq"), axis=0)), "seq", 0, 0
+            ),
+            axis=2,
+        ).reshape(local_len, 3 * width)
         acc_joined = acc_joined + jnp.einsum(
             "td,te->de", row, d_local, preferred_element_type=jnp.float32
         )

time: 2130 us -> 2020 us (0.948)
  local copies, waits for them, and re-layouts: 156 us -> 101 us
  waiting for transfers between devices: 973 us -> 931 us
    all_to_all x2, waiting for transfers between devices: 67 us -> 25.6 us  [micro_step(): lax.all_to_all(jnp.stack(jnp.split(d_joined, lax.axis_size('seq'), axis=0...]
    another operation x6 -> x0, local copies, waits for them, and re-layouts: 31.4 us -> none  [micro_step(): jnp.stack([d_queries, d_keys, d_values], axis=1).astype(jnp.bfloat16)]
where the time goes in v1:
time: 2020 us; the launch traced here: 2010 us
  waiting for transfers between devices  931 us (46%)
  matrix products  724 us (36%)
  other arithmetic  116 us (6%)
  local copies, waits for them, and re-layouts  101 us (5%)
  blocking collectives  91.2 us (5%)
  starting transfers between devices  30.8 us (2%)
    dot_general x8, matrix products, micro_step(): jnp.einsum('hqk,qhd->khd', d_scores, query_block, preferred_element_type=...  205 us
    dot_general x8, matrix products, micro_step(): jnp.einsum('hqk,khd->qhd', d_scores, keys_all, preferred_element_type=jnp...  185 us
    reduce_scatter x1, waiting for transfers between devices, body(): lax.psum_scatter(local_grads[4], 'shard', scatter_dimension=0, tiled=True)  163 us
    reduce_scatter x1, waiting for transfers between devices, body(): lax.psum_scatter(local_grads[6], 'shard', scatter_dimension=0, tiled=True)  163 us
    all_gather x1, waiting for transfers between devices, body(): lax.all_gather(inner_weight, 'shard', axis=0, tiled=True)  80.1 us
    all_gather x1, waiting for transfers between devices, body(): lax.all_gather(outer_weight, 'shard', axis=0, tiled=True)  79.8 us
    reduce_scatter x1, waiting for transfers between devices, body(): lax.psum_scatter(local_grads[0], 'shard', scatter_dimension=0, tiled=True)  70.7 us
    reduce_scatter x1, waiting for transfers between devices, body(): lax.psum_scatter(local_grads[2], 'shard', scatter_dimension=0, tiled=True)  70.6 us
  transfers between devices with their start and end apart: 21, of which 20 were waited for; matrix products, arithmetic and copies ran while one was open for 6% of the time, Pallas kernels for 0%

profile of v1, /device:TPU:0, one launch (start us, length us, event | category | flops | bytes accessed | tf_op | source)
XLA Modules:
  0.0 2014.6 jit_solution(15304259797592893149)
XLA Ops:
  17.3 23.5 %all-reduce.10 = (bf16[768]{0:T(1024)(128)(2,1)S(1)}, bf16[768]{0:T(1024)(128)(2,1)S(1)}, bf16[768]{0:T(1024)(128)(2,1)S(1)}, bf16[768]{0:T(1024)(128)(2,1)S(1)}) all-reduce(bf16[768]{0:T(1024)(128)(2,1)S(1)} %dynamic-update-slice, bf16[768]{0:T(1024)(128)(2,1)S(1)} %dynamic-update-slice.1, ...), channel_id=1, replica_groups=mesh['shard'=8,'seq'=4] {'shard'}, use_global_device_ids=true, to_apply=%add | all-reduce | flops 3072 | bytes 12288
  41.4 26.0 %all-gather = bf16[8,1,384]{2,1,0:T(2,128)(2,1)S(1)} all-gather(bf16[1,1,384]{2,1,0:T(2,128)(2,1)S(1)} %reshape.334), channel_id=1, replica_groups=mesh['shard'=8,'seq'=4] {'shard'}, dimensions={0}, use_global_device_ids=true | all-gather | bytes 6912 | tf_op jit(solution)/shard_map/all_gather | solution.py:72
  67.5 28.6 %all-gather.10.cloned.1.call-done = bf16[768,768]{1,0:T(8,128)(2,1)} async-done(((bf16[96,768]{1,0:T(8,128)(2,1)}), bf16[768,768]{1,0:T(8,128)(2,1)}) %all-gather.10.cloned.1.call-update) | async-done | bytes 1179664 | tf_op jit(solution)/shard_map/all_gather | solution.py:68
  96.1 42.0 %all-gather.12.cloned.1.call-done = bf16[768,768]{1,0:T(8,128)(2,1)} async-done(((bf16[96,768]{1,0:T(8,128)(2,1)}), bf16[768,768]{1,0:T(8,128)(2,1)}) %all-gather.12.cloned.1.call-update) | async-done | bytes 1179664 | tf_op jit(solution)/shard_map/all_gather | solution.py:69
  141.4 38.6 %all-gather.14.cloned.1.call-done = bf16[768,768]{1,0:T(8,128)(2,1)} async-done(((bf16[96,768]{1,0:T(8,128)(2,1)}), bf16[768,768]{1,0:T(8,128)(2,1)}) %all-gather.14.cloned.1.call-update) | async-done | bytes 1179664 | tf_op jit(solution)/shard_map/all_gather | solution.py:70
  180.0 80.1 %all-gather.16.cloned.1.call-done = bf16[768,3072]{1,0:T(8,128)(2,1)} async-done(((bf16[96,3072]{1,0:T(8,128)(2,1)}), bf16[768,3072]{1,0:T(8,128)(2,1)}) %all-gather.16.cloned.1.call-update) | async-done | bytes 4718608 | tf_op jit(solution)/shard_map/all_gather | solution.py:71
  260.1 79.8 %all-gather.18.cloned.1.call-done = bf16[3072,768]{1,0:T(8,128)(2,1)} async-done(((bf16[384,768]{1,0:T(8,128)(2,1)}), bf16[3072,768]{1,0:T(8,128)(2,1)}) %all-gather.18.cloned.1.call-update) | async-done | bytes 4718608 | tf_op jit(solution)/shard_map/all_gather | solution.py:73
  339.8 994.1 %while.34 = (s32[]{:T(128)}, f32[768,2304]{1,0:T(8,128)}, f32[768,768]{1,0:T(8,128)}, f32[768,3072]{1,0:T(8,128)}, f32[3072]{0:T(1024)}, /*index=5*/f32[3072,768...) while((s32[]{:T(128)}, f32[768,2304]{1,0:T(8,128)}, ...), condition=%wide.region_30.31_spmd.clone, body=%wide.region_0.30_spmd.clone.sunk | while | flops 32022925312 | bytes 1231136000 | solution.py:273
  550.0 23.7 %fusion.490 = bf16[512,3,64]{0,2,1:T(8,128)(2,1)} fusion(f32[3,512,2048]{2,1,0:T(8,128)} %fusion.479, f32[3,512,2048]{2,1,0:T(8,128)} %get-tuple-element.927, f32[3,512]{1,0:T(4,128)S(1)} %log_add_fusion.10, pred[512,2048]{1,0:T(8,128)(4,1)} %copy.117, bf16[2048,3,3,64]{0,3,2,1:T(8,128)(2,1)S(1)} %copy-done.1), kind=kOutput, calls=%fused_computation.159.clone.1 | convolution fusion | flops 437358080 | bytes 53428224 | tf_op jit(solution)/shard_map/while/body/eval_jaxpr/hqk,khd->qhd/dot_general | solution.py:229
  573.6 27.8 %fusion.480 = f32[3,64,2048]{2,1,0:T(8,128)} fusion(f32[3,512,2048]{2,1,0:T(8,128)} %fusion.479, f32[3,512,2048]{2,1,0:T(8,128)} %get-tuple-element.927, f32[3,512]{1,0:T(4,128)S(1)} %log_add_fusion.10, pred[512,2048]{1,0:T(8,128)(4,1)} %copy.117, bf16[2048,3,3,64]{0,3,2,1:T(8,128)(2,1)S(1)} %copy-done.1), kind=kOutput, calls=%fused_computation.47.clone.1 | convolution fusion | flops 437259776 | bytes 54214656 | tf_op jit(solution)/shard_map/while/body/eval_jaxpr/hqk,qhd->khd/dot_general | solution.py:231
  643.0 20.7 %fusion.487 = bf16[512,3,64]{0,2,1:T(8,128)(2,1)} fusion(f32[3,512,2048]{2,1,0:T(8,128)} %fusion.485, f32[3,512,2048]{2,1,0:T(8,128)} %get-tuple-element.918, f32[3,512]{1,0:T(4,128)S(1)} %log_add_fusion.11, pred[512,2048]{1,0:T(8,128)(4,1)S(1)} %copy-done.4, bf16[2048,3,3,64]{0,3,2,1:T(8,128)(2,1)S(1)} %copy-done.1), kind=kOutput, calls=%fused_computation.162.clone.1 | convolution fusion | flops 437358080 | bytes 53428224 | tf_op jit(solution)/shard_map/while/body/eval_jaxpr/hqk,khd->qhd/dot_general | solution.py:229
  663.7 23.9 %fusion.488 = bf16[512,3,64]{0,2,1:T(8,128)(2,1)} fusion(f32[3,512,2048]{2,1,0:T(8,128)} %fusion.483, f32[3,512,2048]{2,1,0:T(8,128)} %get-tuple-element.921, f32[3,512]{1,0:T(4,128)S(1)} %log_add_fusion.8, pred[512,2048]{1,0:T(8,128)(4,1)} %copy.115, bf16[2048,3,3,64]{0,3,2,1:T(8,128)(2,1)S(1)} %copy-done.1), kind=kOutput, calls=%fused_computation.161.clone.1 | convolution fusion | flops 437358080 | bytes 53428224 | tf_op jit(solution)/shard_map/while/body/eval_jaxpr/hqk,khd->qhd/dot_general | solution.py:229
  687.6 24.0 %fusion.489 = bf16[512,3,64]{0,2,1:T(8,128)(2,1)} fusion(f32[3,512,2048]{2,1,0:T(8,128)} %fusion.481, f32[3,512,2048]{2,1,0:T(8,128)} %get-tuple-element.924, f32[3,512]{1,0:T(4,128)S(1)} %log_add_fusion.9, pred[512,2048]{1,0:T(8,128)(4,1)} %copy.116, bf16[2048,3,3,64]{0,3,2,1:T(8,128)(2,1)S(1)} %copy-done.1), kind=kOutput, calls=%fused_computation.160.clone.1 | convolution fusion | flops 437358080 | bytes 53428224 | tf_op jit(solution)/shard_map/while/body/eval_jaxpr/hqk,khd->qhd/dot_general | solution.py:229
  711.7 25.9 %fusion.482 = f32[3,64,2048]{2,1,0:T(8,128)} fusion(f32[3,64,2048]{2,1,0:T(8,128)} %fusion.480, f32[3,512,2048]{2,1,0:T(8,128)} %fusion.481, f32[3,512,2048]{2,1,0:T(8,128)} %get-tuple-element.924, f32[3,512]{1,0:T(4,128)S(1)} %log_add_fusion.9, pred[512,2048]{1,0:T(8,128)(4,1)} %copy.116, bf16[2048,3,3,64]{0,3,2,1:T(8,128)(2,1)S(1)} %copy-done.1), kind=kOutput, calls=%fused_computation.117.clone.1 | convolution fusion | flops 437652992 | bytes 55787520 | tf_op jit(solution)/shard_map/while/body/eval_jaxpr/hqk,qhd->khd/dot_general | solution.py:231
  737.5 26.4 %fusion.484 = f32[3,64,2048]{2,1,0:T(8,128)} fusion(f32[3,64,2048]{2,1,0:T(8,128)} %fusion.482, f32[3,512,2048]{2,1,0:T(8,128)} %fusion.483, f32[3,512,2048]{2,1,0:T(8,128)} %get-tuple-element.921, f32[3,512]{1,0:T(4,128)S(1)} %log_add_fusion.8, pred[512,2048]{1,0:T(8,128)(4,1)} %copy.115, bf16[2048,3,3,64]{0,3,2,1:T(8,128)(2,1)S(1)} %copy-done.1), kind=kOutput, calls=%fused_computation.116.clone.1 | convolution fusion | flops 437652992 | bytes 55787520 | tf_op jit(solution)/shard_map/while/body/eval_jaxpr/hqk,qhd->khd/dot_general | solution.py:231
  763.9 22.2 %fusion.486 = bf16[2048,1,3,64]{0,3,2,1:T(8,128)(2,1)} fusion(f32[3,64,2048]{2,1,0:T(8,128)} %fusion.484, f32[3,512,2048]{2,1,0:T(8,128)} %fusion.485, f32[3,512,2048]{2,1,0:T(8,128)} %get-tuple-element.918, f32[3,512]{1,0:T(4,128)S(1)} %log_add_fusion.11, pred[512,2048]{1,0:T(8,128)(4,1)S(1)} %copy-done.4, bf16[2048,3,3,64]{0,3,2,1:T(8,128)(2,1)S(1)} %copy-done.1), kind=kOutput, calls=%fused_computation.121.clone.1 | convolution fusion | flops 438046208 | bytes 55001088 | tf_op jit(solution)/shard_map/while/body/eval_jaxpr/hqk,qhd->khd/dot_general | solution.py:231
  808.8 14.5 all-to-all-done.3
  1044.4 23.7 %fusion.490 = bf16[512,3,64]{0,2,1:T(8,128)(2,1)} fusion(f32[3,512,2048]{2,1,0:T(8,128)} %fusion.479, f32[3,512,2048]{2,1,0:T(8,128)} %get-tuple-element.927, f32[3,512]{1,0:T(4,128)S(1)} %log_add_fusion.10, pred[512,2048]{1,0:T(8,128)(4,1)} %copy.117, bf16[2048,3,3,64]{0,3,2,1:T(8,128)(2,1)S(1)} %copy-done.1), kind=kOutput, calls=%fused_computation.159.clone.1 | convolution fusion | flops 437358080 | bytes 53428224 | tf_op jit(solution)/shard_map/while/body/eval_jaxpr/hqk,khd->qhd/dot_general | solution.py:229
  1068.1 27.8 %fusion.480 = f32[3,64,2048]{2,1,0:T(8,128)} fusion(f32[3,512,2048]{2,1,0:T(8,128)} %fusion.479, f32[3,512,2048]{2,1,0:T(8,128)} %get-tuple-element.927, f32[3,512]{1,0:T(4,128)S(1)} %log_add_fusion.10, pred[512,2048]{1,0:T(8,128)(4,1)} %copy.117, bf16[2048,3,3,64]{0,3,2,1:T(8,128)(2,1)S(1)} %copy-done.1), kind=kOutput, calls=%fused_computation.47.clone.1 | convolution fusion | flops 437259776 | bytes 54214656 | tf_op jit(solution)/shard_map/while/body/eval_jaxpr/hqk,qhd->khd/dot_general | solution.py:231
  1137.4 20.7 %fusion.487 = bf16[512,3,64]{0,2,1:T(8,128)(2,1)} fusion(f32[3,512,2048]{2,1,0:T(8,128)} %fusion.485, f32[3,512,2048]{2,1,0:T(8,128)} %get-tuple-element.918, f32[3,512]{1,0:T(4,128)S(1)} %log_add_fusion.11, pred[512,2048]{1,0:T(8,128)(4,1)S(1)} %copy-done.4, bf16[2048,3,3,64]{0,3,2,1:T(8,128)(2,1)S(1)} %copy-done.1), kind=kOutput, calls=%fused_computation.162.clone.1 | convolution fusion | flops 437358080 | bytes 53428224 | tf_op jit(solution)/shard_map/while/body/eval_jaxpr/hqk,khd->qhd/dot_general | solution.py:229
  1158.1 23.9 %fusion.488 = bf16[512,3,64]{0,2,1:T(8,128)(2,1)} fusion(f32[3,512,2048]{2,1,0:T(8,128)} %fusion.483, f32[3,512,2048]{2,1,0:T(8,128)} %get-tuple-element.921, f32[3,512]{1,0:T(4,128)S(1)} %log_add_fusion.8, pred[512,2048]{1,0:T(8,128)(4,1)} %copy.115, bf16[2048,3,3,64]{0,3,2,1:T(8,128)(2,1)S(1)} %copy-done.1), kind=kOutput, calls=%fused_computation.161.clone.1 | convolution fusion | flops 437358080 | bytes 53428224 | tf_op jit(solution)/shard_map/while/body/eval_jaxpr/hqk,khd->qhd/dot_general | solution.py:229
  1182.1 24.0 %fusion.489 = bf16[512,3,64]{0,2,1:T(8,128)(2,1)} fusion(f32[3,512,2048]{2,1,0:T(8,128)} %fusion.481, f32[3,512,2048]{2,1,0:T(8,128)} %get-tuple-element.924, f32[3,512]{1,0:T(4,128)S(1)} %log_add_fusion.9, pred[512,2048]{1,0:T(8,128)(4,1)} %copy.116, bf16[2048,3,3,64]{0,3,2,1:T(8,128)(2,1)S(1)} %copy-done.1), kind=kOutput, calls=%fused_computation.160.clone.1 | convolution fusion | flops 437358080 | bytes 53428224 | tf_op jit(solution)/shard_map/while/body/eval_jaxpr/hqk,khd->qhd/dot_general | solution.py:229
  1206.1 25.9 %fusion.482 = f32[3,64,2048]{2,1,0:T(8,128)} fusion(f32[3,64,2048]{2,1,0:T(8,128)} %fusion.480, f32[3,512,2048]{2,1,0:T(8,128)} %fusion.481, f32[3,512,2048]{2,1,0:T(8,128)} %get-tuple-element.924, f32[3,512]{1,0:T(4,128)S(1)} %log_add_fusion.9, pred[512,2048]{1,0:T(8,128)(4,1)} %copy.116, bf16[2048,3,3,64]{0,3,2,1:T(8,128)(2,1)S(1)} %copy-done.1), kind=kOutput, calls=%fused_computation.117.clone.1 | convolution fusion | flops 437652992 | bytes 55787520 | tf_op jit(solution)/shard_map/while/body/eval_jaxpr/hqk,qhd->khd/dot_general | solution.py:231
  1232.0 26.4 %fusion.484 = f32[3,64,2048]{2,1,0:T(8,128)} fusion(f32[3,64,2048]{2,1,0:T(8,128)} %fusion.482, f32[3,512,2048]{2,1,0:T(8,128)} %fusion.483, f32[3,512,2048]{2,1,0:T(8,128)} %get-tuple-element.921, f32[3,512]{1,0:T(4,128)S(1)} %log_add_fusion.8, pred[512,2048]{1,0:T(8,128)(4,1)} %copy.115, bf16[2048,3,3,64]{0,3,2,1:T(8,128)(2,1)S(1)} %copy-done.1), kind=kOutput, calls=%fused_computation.116.clone.1 | convolution fusion | flops 437652992 | bytes 55787520 | tf_op jit(solution)/shard_map/while/body/eval_jaxpr/hqk,qhd->khd/dot_general | solution.py:231
  1258.4 22.2 %fusion.486 = bf16[2048,1,3,64]{0,3,2,1:T(8,128)(2,1)} fusion(f32[3,64,2048]{2,1,0:T(8,128)} %fusion.484, f32[3,512,2048]{2,1,0:T(8,128)} %fusion.485, f32[3,512,2048]{2,1,0:T(8,128)} %get-tuple-element.918, f32[3,512]{1,0:T(4,128)S(1)} %log_add_fusion.11, pred[512,2048]{1,0:T(8,128)(4,1)S(1)} %copy-done.4, bf16[2048,3,3,64]{0,3,2,1:T(8,128)(2,1)S(1)} %copy-done.1), kind=kOutput, calls=%fused_computation.121.clone.1 | convolution fusion | flops 438046208 | bytes 55001088 | tf_op jit(solution)/shard_map/while/body/eval_jaxpr/hqk,qhd->khd/dot_general | solution.py:231
  1343.0 58.2 %reduce-scatter.13.cloned.1.call-done = f32[96,768]{1,0:T(8,128)} async-done(((f32[768,768]{1,0:T(8,128)}), f32[96,768]{1,0:T(8,128)}) %reduce-scatter.13.cloned.1.call-update) | async-done | bytes 294928 | tf_op jit(solution)/shard_map/reduce_scatter | solution.py:304
  1402.8 70.6 %reduce-scatter.11.cloned.1.call-done = f32[96,768]{1,0:T(8,128)} async-done(((f32[768,768]{1,0:T(8,128)}), f32[96,768]{1,0:T(8,128)}) %reduce-scatter.11.cloned.1.call-update) | async-done | bytes 294928 | tf_op jit(solution)/shard_map/reduce_scatter | solution.py:303
  1475.1 70.7 %reduce-scatter.7.cloned.1.call-done = f32[96,768]{1,0:T(8,128)} async-done(((f32[768,768]{1,0:T(8,128)}), f32[96,768]{1,0:T(8,128)}) %reduce-scatter.7.cloned.1.call-update) | async-done | bytes 294928 | tf_op jit(solution)/shard_map/reduce_scatter | solution.py:301
  1547.4 70.5 %reduce-scatter.9.cloned.1.call-done = f32[96,768]{1,0:T(8,128)} async-done(((f32[768,768]{1,0:T(8,128)}), f32[96,768]{1,0:T(8,128)}) %reduce-scatter.9.cloned.1.call-update) | async-done | bytes 294928 | tf_op jit(solution)/shard_map/reduce_scatter | solution.py:302
  1619.5 163.3 %reduce-scatter.15.cloned.1.call-done = f32[96,3072]{1,0:T(8,128)} async-done(((f32[768,3072]{1,0:T(8,128)}), f32[96,3072]{1,0:T(8,128)}) %reduce-scatter.15.cloned.1.call-update) | async-done | bytes 1179664 | tf_op jit(solution)/shard_map/reduce_scatter | solution.py:305
  1785.0 162.5 %reduce-scatter.17.cloned.1.call-done = f32[384,768]{1,0:T(8,128)} async-done(((f32[3072,768]{1,0:T(8,128)}), f32[384,768]{1,0:T(8,128)}) %reduce-scatter.17.cloned.1.call-update) | async-done | bytes 1179664 | tf_op jit(solution)/shard_map/reduce_scatter | solution.py:307
  1951.0 35.2 %all-reduce.9 = (bf16[3072]{0:T(1024)(128)(2,1)S(1)}, bf16[768]{0:T(1024)(128)(2,1)S(1)}, bf16[768]{0:T(1024)(128)(2,1)S(1)}, bf16[768]{0:T(1024)(128)(2,1)S(1)}, bf16[768]{0:T(1024)(128)(2,1)S(1)}) all-reduce(f32[3072]{0:T(1024)S(1)} %copy-done.25, f32[768]{0:T(1024)S(1)} %copy-done.39, ...), channel_id=7, replica_groups=mesh['shard'=8,'seq'=4] {'shard'}, use_global_device_ids=true, to_apply=%region_41.42.clone | all-reduce | flops 6144 | bytes 36864
  (486 shorter events, 640.4 us)
Async XLA Ops:
  7.2 332.7 %copy-start.21 = (bf16[2,512,768]{2,1,0:T(8,128)(2,1)S(1)}, bf16[2,512,768]{2,1,0:T(8,128)(2,1)}, u32[]{:S(2)}) copy-start(bf16[2,512,768]{2,1,0:T(8,128)(2,1)} %param.17) | copy-start | bytes 4718596
  7.2 60.3 %all-gather.8.cloned.1.call-start = ((), (), s32[]{:S(2)}) async-start(), calls=%async_computation.10 | async-start | bytes 1327104 | tf_op jit(solution)/shard_map/all_gather | solution.py:67
  7.9 88.2 %all-gather.10.cloned.1.call-start = ((), (), s32[]{:S(2)}) async-start(), calls=%async_computation.11 | async-start | bytes 1327104 | tf_op jit(solution)/shard_map/all_gather | solution.py:68
  8.7 129.4 %all-gather.12.cloned.1.call-start = ((), (), s32[]{:S(2)}) async-start(), calls=%async_computation.12 | async-start | bytes 1327104 | tf_op jit(solution)/shard_map/all_gather | solution.py:69
  9.4 170.6 %all-gather.14.cloned.1.call-start = ((), (), s32[]{:S(2)}) async-start(), calls=%async_computation.13 | async-start | bytes 1327104 | tf_op jit(solution)/shard_map/all_gather | solution.py:70
  10.0 250.1 %all-gather.16.cloned.1.call-start = ((), (), s32[]{:S(2)}) async-start(), calls=%async_computation.14 | async-start | bytes 5308416 | tf_op jit(solution)/shard_map/all_gather | solution.py:71
  10.6 329.3 %all-gather.18.cloned.1.call-start = ((), (), s32[]{:S(2)}) async-start(), calls=%async_computation.15 | async-start | bytes 5308416 | tf_op jit(solution)/shard_map/all_gather | solution.py:73
  11.1 1390.0 %reduce-scatter.13.cloned.1.call-start = ((), (), s32[]{:S(2)}) async-start(), calls=%async_computation.19 | async-start | bytes 2654208 | tf_op jit(solution)/shard_map/reduce_scatter | solution.py:304
  349.8 32.1 %all-to-all-start = ((bf16[512,3,4,192]{0,3,1,2:T(8,128)(2,1)}), bf16[512,3,4,192]{0,3,1,2:T(8,128)(2,1)S(1)}, u32[]{:S(2)}, u32[]{:S(2)}) async-start(bf16[512,3,4,192]{0,3,1,2:T(8,128)(2,1)} %copy.113), calls=%async_computation | async-start | bytes 4718592 | tf_op jit(solution)/shard_map/while/body/eval_jaxpr/all_to_all | solution.py:126
  365.4 97.6 %copy-start.3 = (pred[512,2048]{1,0:T(8,128)(4,1)}, pred[512,2048]{1,0:T(8,128)(4,1)S(1)}, u32[]{:S(2)}) copy-start(pred[512,2048]{1,0:T(8,128)(4,1)S(1)} %copy.111) | copy-start | bytes 3145732 | tf_op jit(solution)/shard_map/while
  474.4 15.1 all-to-all-start.1
  524.5 15.9 all-to-all-start.2
  541.7 82.8 %copy-start.17 = (bf16[1,512,1,192]{1,3,0,2:T(8,128)(2,1)}, bf16[1,512,1,192]{1,3,0,2:T(8,128)(2,1)S(1)}, u32[]{:S(2)}) copy-start(bf16[1,512,1,192]{1,3,0,2:T(8,128)(2,1)S(1)} %get-tuple-element.944) | copy-start | bytes 589828 | tf_op jit(solution)/shard_map/while
  791.1 32.2 %all-to-all-start.3 = ((bf16[4,512,3,1,192]{1,4,2,3,0:T(8,128)(2,1)}), bf16[4,512,3,1,192]{1,4,2,3,0:T(8,128)(2,1)S(1)}, u32[]{:S(2)}, u32[]{:S(2)}) async-start(bf16[4,512,3,1,192]{1,4,2,3,0:T(8,128)(2,1)} %pad_maximum_fusion.9), calls=%async_computation.3 | async-start | bytes 4718592 | tf_op jit(solution)/shard_map/while/body/eval_jaxpr/all_to_all | solution.py:238
  844.2 32.1 %all-to-all-start = ((bf16[512,3,4,192]{0,3,1,2:T(8,128)(2,1)}), bf16[512,3,4,192]{0,3,1,2:T(8,128)(2,1)S(1)}, u32[]{:S(2)}, u32[]{:S(2)}) async-start(bf16[512,3,4,192]{0,3,1,2:T(8,128)(2,1)} %copy.113), calls=%async_computation | async-start | bytes 4718592 | tf_op jit(solution)/shard_map/while/body/eval_jaxpr/all_to_all | solution.py:126
  859.9 97.6 %copy-start.3 = (pred[512,2048]{1,0:T(8,128)(4,1)}, pred[512,2048]{1,0:T(8,128)(4,1)S(1)}, u32[]{:S(2)}) copy-start(pred[512,2048]{1,0:T(8,128)(4,1)S(1)} %copy.111) | copy-start | bytes 3145732 | tf_op jit(solution)/shard_map/while
  884.3 73.2 %copy-start = (bf16[2048,3,3,64]{0,3,2,1:T(8,128)(2,1)}, bf16[2048,3,3,64]{0,3,2,1:T(8,128)(2,1)S(1)}, u32[]{:S(2)}) copy-start(bf16[2048,3,3,64]{0,3,2,1:T(8,128)(2,1)S(1)} %reshape.366) | copy-start | bytes 7077892 | tf_op jit(solution)/shard_map/while
  968.9 15.1 all-to-all-start.1
  1018.9 15.9 all-to-all-start.2
  1036.1 82.8 %copy-start.17 = (bf16[1,512,1,192]{1,3,0,2:T(8,128)(2,1)}, bf16[1,512,1,192]{1,3,0,2:T(8,128)(2,1)S(1)}, u32[]{:S(2)}) copy-start(bf16[1,512,1,192]{1,3,0,2:T(8,128)(2,1)S(1)} %get-tuple-element.944) | copy-start | bytes 589828 | tf_op jit(solution)/shard_map/while
  1285.5 32.2 %all-to-all-start.3 = ((bf16[4,512,3,1,192]{1,4,2,3,0:T(8,128)(2,1)}), bf16[4,512,3,1,192]{1,4,2,3,0:T(8,128)(2,1)S(1)}, u32[]{:S(2)}, u32[]{:S(2)}) async-start(bf16[4,512,3,1,192]{1,4,2,3,0:T(8,128)(2,1)} %pad_maximum_fusion.9), calls=%async_computation.3 | async-start | bytes 4718592 | tf_op jit(solution)/shard_map/while/body/eval_jaxpr/all_to_all | solution.py:238
  1334.0 139.4 %reduce-scatter.11.cloned.1.call-start = ((), (), s32[]{:S(2)}) async-start(), calls=%async_computation.18 | async-start | bytes 2654208 | tf_op jit(solution)/shard_map/reduce_scatter | solution.py:303
  1340.3 205.4 %reduce-scatter.7.cloned.1.call-start = ((), (), s32[]{:S(2)}) async-start(), calls=%async_computation.16 | async-start | bytes 2654208 | tf_op jit(solution)/shard_map/reduce_scatter | solution.py:301
  1341.0 276.8 %reduce-scatter.9.cloned.1.call-start = ((), (), s32[]{:S(2)}) async-start(), calls=%async_computation.17 | async-start | bytes 2654208 | tf_op jit(solution)/shard_map/reduce_scatter | solution.py:302
  1341.6 441.2 %reduce-scatter.15.cloned.1.call-start = ((), (), s32[]{:S(2)}) async-start(), calls=%async_computation.20 | async-start | bytes 10616832 | tf_op jit(solution)/shard_map/reduce_scatter | solution.py:305
  1342.4 605.1 %reduce-scatter.17.cloned.1.call-start = ((), (), s32[]{:S(2)}) async-start(), calls=%async_computation.21 | async-start | bytes 10616832 | tf_op jit(solution)/shard_map/reduce_scatter | solution.py:307
  1342.4 608.6 %copy-start.25 = (f32[3072]{0:T(1024)S(1)}, f32[3072]{0:T(1024)}, u32[]{:S(2)}) copy-start(f32[3072]{0:T(1024)} %get-tuple-element.1085) | copy-start | bytes 36868
  1342.4 608.6 %copy-start.30 = (f32[768]{0:T(1024)S(1)}, f32[768]{0:T(1024)}, u32[]{:S(2)}) copy-start(f32[768]{0:T(1024)} %get-tuple-element.1090) | copy-start | bytes 9220
  1342.4 608.6 %copy-start.33 = (f32[768]{0:T(1024)S(1)}, f32[768]{0:T(1024)}, u32[]{:S(2)}) copy-start(f32[768]{0:T(1024)} %get-tuple-element.1089) | copy-start | bytes 9220
  1342.4 608.6 %copy-start.36 = (f32[768]{0:T(1024)S(1)}, f32[768]{0:T(1024)}, u32[]{:S(2)}) copy-start(f32[768]{0:T(1024)} %get-tuple-element.1088) | copy-start | bytes 9220
  1342.4 608.6 %copy-start.39 = (f32[768]{0:T(1024)S(1)}, f32[768]{0:T(1024)}, u32[]{:S(2)}) copy-start(f32[768]{0:T(1024)} %get-tuple-element.1087) | copy-start | bytes 9220
  1342.9 653.9 %all-reduce.15.cloned.1.call-start = ((), (), s32[]{:S(2)}) async-start(), calls=%async_computation.22 | async-start | bytes 3538944 | tf_op jit(solution)/shard_map/psum | solution.py:314
  (87 other events, 761.9 us)
Sparse Core Ops, SparseCore 0:
  10.2 43.8 all-gather.7
  56.2 39.8 all-gather.9
  98.3 39.8 all-gather.11
  140.1 39.8 all-gather.13
  182.0 78.0 all-gather.15
  262.1 77.6 all-gather.17
  1334.1 67.0 reduce-scatter.12
  1404.7 68.7 reduce-scatter.10
  1476.9 68.7 reduce-scatter.6
  1549.1 68.7 reduce-scatter.8
  1621.5 161.2 reduce-scatter.14
  1786.3 161.1 reduce-scatter.16
  1951.4 45.3 all-reduce.14
